TPU v7x, 32 devices: a whole 2x2x4 slice. The times are simulated.
32 devices in a mesh: gx: 2 (over y), gy: 4 (over x, core), gz: 4 (over z).
Axes of the slice: x: 2, y: 2, z: 4, core: 2. Of those that a mesh axis runs over, the one named last changes fastest.
Arguments:
- direction: float32 [3, 32, 32, 512], P(None, 'gx', 'gy', 'gz'), may hold values from -6 to 6
- base_flow: bfloat16 [2, 3, 32, 32, 512], P(None, None, 'gx', 'gy', 'gz'), may hold values from -4 to 4
- local_inv: float32 [32, 16], P('gx'), may hold values from -1.5 to 1.5
- couple_in: float32 [4, 16], P('gx'), may hold values from -1.5 to 1.5
- couple_out: float32 [32, 2], P('gx'), may hold values from -4 to 4
- schur_inv: float32 [4, 4], replicated, may hold values from -3 to 3
- plane_x: int32 [8], replicated, may hold values from 0 to 31, as said below
- slot_plane: int32 [8], replicated, may hold values from 0 to 7, each once
- window_inv: float32 [8, 4, 4, 16, 16], P('gx', 'gy', 'gz'), may hold values from -4 to 20
Outputs:
- hess_vec: float32 [3, 32, 32, 512], P(None, 'gx', 'gy', 'gz')
Inputs may be any that keep to these rules, and one draw needn't show every extreme that they name: `plane_x`: each plane lies on a streamwise cell of the grid; the planes lie on distinct cells; at most 8 of them lie in the cells of one index d of gx (cells d*16 to d*16 + 15), and some index holds exactly 8.
All inputs are finite; a program needn't handle non-finite values.
Results may differ from a plain program's by a relative error of at most 0.0003.
Values sent between devices are 32-bit elements; how exact they have to be, the bound alone decides.
A program may use at most 64 MiB of HBM per device.

v0:
```python
import jax
import jax.numpy as jnp
from jax import lax
from jax.sharding import PartitionSpec as P

WIN = 8


time_step = 0.15
high = lax.Precision.HIGHEST


def extended(cells, sides, width, closed):
    for axis, dim in sides:
        count = lax.axis_size(axis)
        ends = count if closed else count - 1
        head = lax.slice_in_dim(cells, 0, width, axis=dim)
        tail = lax.slice_in_dim(cells, cells.shape[dim] - width, cells.shape[dim], axis=dim)
        cells = jnp.concatenate(
            [
                lax.ppermute(tail, axis, [(i, (i + 1) % count) for i in range(ends)]),
                cells,
                lax.ppermute(head, axis, [((i + 1) % count, i) for i in range(ends)]),
            ],
            axis=dim,
        )
    return cells


def stencil_x(field):
    length = field.shape[1]
    padded = extended(field, (("gx", 1),), 2, False)
    near_diff = padded[:, 3 : length + 3] - padded[:, 1 : length + 1]
    far_diff = padded[:, 4 : length + 4] - padded[:, 0:length]
    return 7.0 / 9.0 * near_diff + 1.0 / 36.0 * far_diff


def cross_padded(field):
    return extended(field, (("gy", 2), ("gz", 3)), 3, True)


def sixth_order(minus_one, plus_one, minus_two, plus_two, minus_three, plus_three):
    return (
        45.0 * (plus_one - minus_one) - 9.0 * (plus_two - minus_two) + (plus_three - minus_three)
    ) / 60.0


def along_y(padded):
    height = padded.shape[2] - 6
    middle = padded[:, :, :, 3 : padded.shape[3] - 3]

    def taken(offset):
        return middle[:, :, 3 + offset : 3 + offset + height]

    return sixth_order(taken(-1), taken(1), taken(-2), taken(2), taken(-3), taken(3))


def along_z(padded):
    breadth = padded.shape[3] - 6
    middle = padded[:, :, 3 : padded.shape[2] - 3, :]

    def taken(offset):
        return middle[:, :, :, 3 + offset : 3 + offset + breadth]

    return sixth_order(taken(-1), taken(1), taken(-2), taken(2), taken(-3), taken(3))


def interface_sum(edge_values, weight_cols):
    return jnp.einsum(
        "ma,mcyz->acyz",
        weight_cols,
        lax.all_gather(edge_values, "gx", axis=0, tiled=True),
        precision=high,
    )


def local(
    direction,
    base_flow,
    local_inv,
    couple_in,
    couple_out,
    schur_inv,
    plane_x,
    slot_plane,
    window_inv,
):
    gx_index = lax.axis_index("gx")
    holders = lax.axis_size("gx")
    x_cells = direction.shape[1]
    planes = plane_x.shape[0]
    owned_slots = window_inv.shape[0]
    window_count = window_inv.shape[3]
    hold_most = min(planes, 3 * owned_slots)
    own_rows = lax.dynamic_slice_in_dim(schur_inv, 2 * gx_index, 2, 0)
    own_cols = lax.dynamic_slice_in_dim(schur_inv, 2 * gx_index, 2, 1)

    def solve_x(rhs):
        local_part = jnp.einsum("ij,cjyz->ciyz", local_inv, rhs, precision=high)
        edge_values = jnp.einsum("kj,cjyz->kcyz", couple_in, rhs, precision=high)
        solved = interface_sum(edge_values, jnp.transpose(own_rows))
        return local_part + jnp.einsum("ik,kcyz->ciyz", couple_out, solved, precision=high)

    def solve_x_adjoint(grad_in):
        local_part = jnp.einsum("ji,cjyz->ciyz", local_inv, grad_in, precision=high)
        edge_values = jnp.einsum("ik,ciyz->kcyz", couple_out, grad_in, precision=high)
        solved = interface_sum(edge_values, own_cols)
        return local_part + jnp.einsum("ki,kcyz->ciyz", couple_in, solved, precision=high)

    owner_of = plane_x // x_cells
    device_hot = (owner_of[None, :] == jnp.arange(holders, dtype=jnp.int32)[:, None]).astype(
        jnp.int32
    )
    ranks = jnp.cumsum(device_hot, axis=1) - 1
    slot_range = jnp.arange(hold_most, dtype=jnp.int32)[None, :, None]
    pick_all = ((device_hot[:, None, :] == 1) & (ranks[:, None, :] == slot_range)).astype(
        jnp.float32
    )
    pick_own = lax.dynamic_index_in_dim(pick_all, gx_index, 0, keepdims=False)
    local_x = plane_x - gx_index * x_cells
    slot_x = jnp.sum(jnp.where(pick_own > 0, local_x[None, :], 0), axis=1)
    filled = jnp.sum(pick_own, axis=1) > 0
    cell_range = jnp.arange(x_cells, dtype=jnp.int32)[None, :]
    select = (filled[:, None] & (slot_x[:, None] == cell_range)).astype(jnp.float32)
    plane_slot = (slot_plane[:, None] == jnp.arange(planes, dtype=jnp.int32)[None, :]).astype(
        jnp.float32
    )
    route = jnp.dot(pick_own, jnp.transpose(plane_slot), precision=high)
    inverse_here = window_inv.reshape(owned_slots, window_count, window_count)

    def windows_of(state):
        plane_rows = jnp.einsum("sx,cxyz->scyz", select, state, precision=high)
        return plane_rows.reshape(
            plane_rows.shape[0], 3, plane_rows.shape[2], plane_rows.shape[3] // WIN, WIN
        ).mean(axis=4)

    def spread_back(weighted):
        expanded = jnp.repeat(weighted, WIN, axis=3) / WIN
        return jnp.einsum("sx,scyz->cxyz", select, expanded, precision=high)

    every_inv = lax.all_gather(inverse_here, "gx", axis=0, tiled=True)
    held_inv = jnp.einsum("sj,jab->sab", route, every_inv, precision=high)

    def observe(state):
        weighted = jnp.einsum("sab,scyb->scya", held_inv, windows_of(state), precision=high)
        return spread_back(weighted)

    def tangent(state, step_base):
        velocity = step_base.astype(jnp.float32)
        slope_x = solve_x(stencil_x(state))
        padded = cross_padded(state)
        return state - time_step * (
            velocity[0] * slope_x + velocity[1] * along_y(padded) + velocity[2] * along_z(padded)
        )

    def adjoint(state, step_base):
        velocity = step_base.astype(jnp.float32)
        pulled = stencil_x(solve_x_adjoint(velocity[0] * state))
        padded = cross_padded(jnp.concatenate([velocity[1] * state, velocity[2] * state], axis=0))
        return state + time_step * (pulled + along_y(padded[:3]) + along_z(padded[3:]))

    state_one = tangent(direction, base_flow[0])
    state_two = tangent(state_one, base_flow[1])
    adjoint_two = observe(state_two)
    adjoint_one = adjoint(adjoint_two, base_flow[1]) + observe(state_one)
    return adjoint(adjoint_one, base_flow[0]) + direction


def solution(mesh):
    return jax.shard_map(
        local,
        mesh=mesh,
        in_specs=(
            P(None, "gx", "gy", "gz"),
            P(None, None, "gx", "gy", "gz"),
            P("gx", None),
            P("gx", None),
            P("gx", None),
            P(),
            P(),
            P(),
            P("gx", "gy", "gz", None, None),
        ),
        out_specs=P(None, "gx", "gy", "gz"),
        check_vma=False,
    )
```

profile of v0, /device:TPU:0, one launch (start us, length us, event | category | flops | bytes accessed | tf_op | source)
XLA Modules:
  0.0 129.9 jit_solution(2365292226690273208)
XLA Ops:
  0.0 1.0 copy.84
  1.6 2.0 %collective-permute-start.2 = (f32[3,16,3,128]{3,1,2,0:T(8,128)S(1)}, f32[3,16,3,128]{3,1,2,0:T(8,128)S(1)}, u32[]{:S(2)}, u32[]{:S(2)}) collective-permute-start(f32[3,16,3,128]{3,1,2,0:T(8,128)S(1)} %get-tuple-element.51), channel_id=1, source_target_pairs={{4,0},{8,4},{12,8},{0,12},{5,1},{9,5},{13,9},{1,13},{6,2},{10,6},{... | collective-permute-start | bytes 221192 | tf_op jit(solution)/shard_map/ppermute | solution.py:23
  3.6 4.2 %collective-permute-start.1 = (f32[3,2,8,128]{3,1,2,0:T(2,128)S(1)}, f32[3,2,8,128]{3,1,2,0:T(2,128)S(1)}, u32[]{:S(2)}, u32[]{:S(2)}) collective-permute-start(f32[3,2,8,128]{3,1,2,0:T(2,128)S(1)} %get-tuple-element.44), channel_id=1, source_target_pairs={{0,16},{1,17},{2,18},{3,19},{4,20},{5,21},{6,22},{7,23},{8,24},{9,... | collective-permute-start | bytes 73736 | tf_op jit(solution)/shard_map/ppermute | solution.py:21
  7.8 1.3 collective-permute-start
  9.1 1.0 slice_convert_fusion
  12.0 5.2 %all-gather = f32[8,1,1,16,16]{4,3,2,1,0:T(8,128)S(1)} all-gather(f32[4,1,1,16,16]{4,3,2,1,0:T(8,128)S(1)} %copy-done.4), channel_id=2, replica_groups=mesh['gx'=2,'gy'=4,'gz'=4] {'gx'}, dimensions={0}, use_global_device_ids=true | all-gather | bytes 12288 | tf_op jit(solution)/shard_map/all_gather | solution.py:141
  18.0 1.6 %collective-permute-start.5 = (f32[3,16,14,3]{3,1,2,0:T(8,128)S(1)}, f32[3,16,14,3]{3,1,2,0:T(8,128)S(1)}, u32[]{:S(2)}, u32[]{:S(2)}) collective-permute-start(f32[3,16,14,3]{3,1,2,0:T(8,128)S(1)} %get-tuple-element.20), channel_id=1, source_target_pairs={{0,1},{1,2},{2,3},{3,0},{4,5},{5,6},{6,7},{7,4},{8,9},{9,10},{10,1... | collective-permute-start | bytes 24200 | tf_op jit(solution)/shard_map/ppermute | solution.py:21
  19.6 2.2 %collective-permute-start.4 = (f32[3,16,14,3]{3,1,2,0:T(8,128)S(1)}, f32[3,16,14,3]{3,1,2,0:T(8,128)S(1)}, u32[]{:S(2)}, u32[]{:S(2)}) collective-permute-start(f32[3,16,14,3]{3,1,2,0:T(8,128)S(1)} %get-tuple-element.19), channel_id=1, source_target_pairs={{1,0},{2,1},{3,2},{0,3},{5,4},{6,5},{7,6},{4,7},{9,8},{10,9},{11,1... | collective-permute-start | bytes 24200 | tf_op jit(solution)/shard_map/ppermute | solution.py:23
  22.6 4.5 %all_gather.15 = f32[4,3,8,128]{3,2,1,0:T(8,128)S(1)} all-gather(f32[2,3,8,128]{3,2,1,0:T(8,128)S(1)} %copy.75), channel_id=1, replica_groups=mesh['gx'=2,'gy'=4,'gz'=4] {'gx'}, dimensions={0}, use_global_device_ids=true | all-gather | bytes 73728 | tf_op jit(solution)/shard_map/all_gather | solution.py:72
  27.3 3.5 %collective-permute-done.5 = f32[3,16,14,3]{3,1,2,0:T(8,128)S(1)} collective-permute-done((f32[3,16,14,3]{3,1,2,0:T(8,128)S(1)}, f32[3,16,14,3]{3,1,2,0:T(8,128)S(1)}, u32[]{:S(2)}, u32[]{:S(2)}) %collective-permute-start.5) | collective-permute-done | bytes 8096 | tf_op jit(solution)/shard_map/ppermute | solution.py:21
  30.8 4.3 %collective-permute-done.4 = f32[3,16,14,3]{3,1,2,0:T(8,128)S(1)} collective-permute-done((f32[3,16,14,3]{3,1,2,0:T(8,128)S(1)}, f32[3,16,14,3]{3,1,2,0:T(8,128)S(1)}, u32[]{:S(2)}, u32[]{:S(2)}) %collective-permute-start.4) | collective-permute-done | bytes 8096 | tf_op jit(solution)/shard_map/ppermute | solution.py:23
  35.1 0.8 fusion.90
  36.2 0.8 reshape.79
  37.0 3.7 %collective-permute-start.7 = (f32[3,2,8,128]{3,1,2,0:T(2,128)S(1)}, f32[3,2,8,128]{3,1,2,0:T(2,128)S(1)}, u32[]{:S(2)}, u32[]{:S(2)}) collective-permute-start(f32[3,2,8,128]{3,1,2,0:T(2,128)S(1)} %get-tuple-element.42), channel_id=1, source_target_pairs={{0,16},{1,17},{2,18},{3,19},{4,20},{5,21},{6,22},{7,23},{8,24},{9,... | collective-permute-start | bytes 73736 | tf_op jit(solution)/shard_map/ppermute | solution.py:21
  40.7 1.3 collective-permute-start.6
  43.3 0.8 div.55
  44.1 1.7 %collective-permute-start.8 = (f32[3,16,3,128]{3,1,2,0:T(8,128)S(1)}, f32[3,16,3,128]{3,1,2,0:T(8,128)S(1)}, u32[]{:S(2)}, u32[]{:S(2)}) collective-permute-start(f32[3,16,3,128]{3,1,2,0:T(8,128)S(1)} %get-tuple-element.37), channel_id=1, source_target_pairs={{4,0},{8,4},{12,8},{0,12},{5,1},{9,5},{13,9},{1,13},{6,2},{10,6},{... | collective-permute-start | bytes 221192 | tf_op jit(solution)/shard_map/ppermute | solution.py:23
  47.1 4.5 %all_gather.16 = f32[4,3,8,128]{3,2,1,0:T(8,128)S(1)} all-gather(f32[2,3,8,128]{3,2,1,0:T(8,128)S(1)} %copy.86), channel_id=1, replica_groups=mesh['gx'=2,'gy'=4,'gz'=4] {'gx'}, dimensions={0}, use_global_device_ids=true | all-gather | bytes 73728 | tf_op jit(solution)/shard_map/all_gather | solution.py:72
  52.1 1.2 collective-permute-start.11
  53.3 2.7 %collective-permute-start.10 = (f32[3,16,14,3]{3,1,2,0:T(8,128)S(1)}, f32[3,16,14,3]{3,1,2,0:T(8,128)S(1)}, u32[]{:S(2)}, u32[]{:S(2)}) collective-permute-start(f32[3,16,14,3]{3,1,2,0:T(8,128)S(1)} %get-tuple-element.17), channel_id=1, source_target_pairs={{1,0},{2,1},{3,2},{0,3},{5,4},{6,5},{7,6},{4,7},{9,8},{10,9},{11,1... | collective-permute-start | bytes 24200 | tf_op jit(solution)/shard_map/ppermute | solution.py:23
  56.3 8.5 %collective-permute-done.11 = f32[3,16,14,3]{3,1,2,0:T(8,128)S(1)} collective-permute-done((f32[3,16,14,3]{3,1,2,0:T(8,128)S(1)}, f32[3,16,14,3]{3,1,2,0:T(8,128)S(1)}, u32[]{:S(2)}, u32[]{:S(2)}) %collective-permute-start.11) | collective-permute-done | bytes 8096 | tf_op jit(solution)/shard_map/ppermute | solution.py:21
  64.9 3.5 %collective-permute-done.10 = f32[3,16,14,3]{3,1,2,0:T(8,128)S(1)} collective-permute-done((f32[3,16,14,3]{3,1,2,0:T(8,128)S(1)}, f32[3,16,14,3]{3,1,2,0:T(8,128)S(1)}, u32[]{:S(2)}, u32[]{:S(2)}) %collective-permute-start.10) | collective-permute-done | bytes 8096 | tf_op jit(solution)/shard_map/ppermute | solution.py:23
  68.4 0.8 fusion.102
  69.2 0.8 reshape.77
  71.3 0.8 div.50
  73.7 4.6 %all_gather.18 = f32[4,3,8,128]{3,2,1,0:T(8,128)S(1)} all-gather(f32[2,3,8,128]{3,2,1,0:T(8,128)S(1)} %copy.96), channel_id=1, replica_groups=mesh['gx'=2,'gy'=4,'gz'=4] {'gx'}, dimensions={0}, use_global_device_ids=true | all-gather | bytes 73728 | tf_op jit(solution)/shard_map/all_gather | solution.py:72
  79.0 3.7 %collective-permute-start.13 = (f32[3,2,8,128]{3,1,2,0:T(2,128)S(1)}, f32[3,2,8,128]{3,1,2,0:T(2,128)S(1)}, u32[]{:S(2)}, u32[]{:S(2)}) collective-permute-start(f32[3,2,8,128]{3,1,2,0:T(2,128)S(1)} %get-tuple-element.34), channel_id=1, source_target_pairs={{0,16},{1,17},{2,18},{3,19},{4,20},{5,21},{6,22},{7,23},{8,24},{9,... | collective-permute-start | bytes 73736 | tf_op jit(solution)/shard_map/ppermute | solution.py:21
  82.6 1.3 collective-permute-start.12
  85.0 1.0 collective-permute-start.17
  86.7 3.1 %collective-permute-start.16 = (f32[6,16,14,3]{2,1,3,0:T(8,128)S(1)}, f32[6,16,14,3]{2,1,3,0:T(8,128)}, u32[]{:S(2)}, u32[]{:S(2)}) collective-permute-start(f32[6,16,14,3]{2,1,3,0:T(8,128)S(1)} %copy.100), channel_id=1, source_target_pairs={{1,0},{2,1},{3,2},{0,3},{5,4},{6,5},{7,6},{4,7},{9,8},{10,9},{11,1... | collective-permute-start | bytes 48392 | tf_op jit(solution)/shard_map/ppermute | solution.py:23
  89.8 1.1 pad_maximum_fusion.2
  90.9 2.9 %collective-permute-done.17 = f32[6,16,14,3]{2,1,3,0:T(8,128)S(1)} collective-permute-done((f32[6,16,14,3]{2,1,3,0:T(8,128)S(1)}, f32[6,16,14,3]{2,1,3,0:T(8,128)S(1)}, u32[]{:S(2)}, u32[]{:S(2)}) %collective-permute-start.17) | collective-permute-done | bytes 16160 | tf_op jit(solution)/shard_map/ppermute | solution.py:21
  93.8 0.8 copy.103
  94.5 1.0 collective-permute-done.16
  95.5 1.7 %copy.101 = f32[6,16,14,3]{3,1,2,0:T(8,128)S(1)} copy(f32[6,16,14,3]{2,1,3,0:T(8,128)} %collective-permute-done.16) | data formatting | bytes 32256 | tf_op jit(solution)/shard_map/ppermute | solution.py:23
  97.8 2.1 %broadcast_multiply_fusion.1 = (f32[3,16,8,128]{3,1,2,0:T(8,128)S(1)}, f32[3,16,8,128]{3,1,2,0:T(8,128)S(1)}, f32[3,16,8,128]{3,1,2,0:T(8,128)S(1)}) fusion(f32[16,8,128]{2,0,1:T(8,128)S(1)} %copy-done.3, f32[16,8,128]{2,0,1:T(8,128)} %copy.111, s32[8]{0:T(128)S(1)} %copy-done.10, pred[8]{0:T(512)(128)(4,1)S(1)} %copy-done.12, ...), kind=kOutput, calls=%fused_computation.209 | convolution fusion | flops 7471360 | bytes 3161640 | tf_op jit(solution)/shard_map/sx,scyz->cxyz/dot_general | solution.py:139
  100.6 4.8 %all_gather.19 = f32[4,3,8,128]{3,2,1,0:T(8,128)S(1)} all-gather(f32[2,3,8,128]{3,2,1,0:T(8,128)S(1)} %copy.108), channel_id=1, replica_groups=mesh['gx'=2,'gy'=4,'gz'=4] {'gx'}, dimensions={0}, use_global_device_ids=true | all-gather | bytes 73728 | tf_op jit(solution)/shard_map/all_gather | solution.py:72
  107.4 4.5 %collective-permute-start.19 = (f32[3,2,8,128]{3,1,2,0:T(2,128)}, f32[3,2,8,128]{3,1,2,0:T(2,128)}, u32[]{:S(2)}, u32[]{:S(2)}) collective-permute-start(f32[3,2,8,128]{3,1,2,0:T(2,128)} %get-tuple-element.27), channel_id=1, source_target_pairs={{0,16},{1,17},{2,18},{3,19},{4,20},{5,21},{6,22},{7,23},{8,24},{9,... | collective-permute-start | bytes 73736 | tf_op jit(solution)/shard_map/ppermute | solution.py:21
  111.9 1.3 collective-permute-start.18
  113.6 1.4 %copy.114 = f32[6,16,14,3]{2,1,3,0:T(8,128)} copy(f32[6,16,14,3]{3,1,2,0:T(8,128)S(1)} %get-tuple-element.6) | data formatting | bytes 32256 | tf_op jit(solution)/shard_map/slice | solution.py:18
  115.0 1.1 collective-permute-start.23
  116.8 2.8 %collective-permute-start.22 = (f32[6,16,14,3]{2,1,3,0:T(8,128)S(1)}, f32[6,16,14,3]{2,1,3,0:T(8,128)}, u32[]{:S(2)}, u32[]{:S(2)}) collective-permute-start(f32[6,16,14,3]{2,1,3,0:T(8,128)S(1)} %copy.112), channel_id=1, source_target_pairs={{1,0},{2,1},{3,2},{0,3},{5,4},{6,5},{7,6},{4,7},{9,8},{10,9},{11,1... | collective-permute-start | bytes 48392 | tf_op jit(solution)/shard_map/ppermute | solution.py:23
  119.6 4.1 %collective-permute-done.23 = f32[6,16,14,3]{2,1,3,0:T(8,128)S(1)} collective-permute-done((f32[6,16,14,3]{2,1,3,0:T(8,128)}, f32[6,16,14,3]{2,1,3,0:T(8,128)S(1)}, u32[]{:S(2)}, u32[]{:S(2)}) %collective-permute-start.23) | collective-permute-done | bytes 16160 | tf_op jit(solution)/shard_map/ppermute | solution.py:21
  123.7 0.8 copy.115
  124.5 1.0 collective-permute-done.22
  125.5 1.7 %copy.113 = f32[6,16,14,3]{3,1,2,0:T(8,128)S(1)} copy(f32[6,16,14,3]{2,1,3,0:T(8,128)} %collective-permute-done.22) | data formatting | bytes 32256 | tf_op jit(solution)/shard_map/ppermute | solution.py:23
  127.2 1.9 %fusion.30 = f32[3,16,8,128]{3,1,2,0:T(8,128)S(1)} fusion(f32[3,16,8,128]{3,1,2,0:T(8,128)S(1)} %get-tuple-element.62, f32[3,2,8,128]{3,1,2,0:T(2,128)} %collective-permute-done.19, f32[3,16,8,128]{3,1,2,0:T(8,128)} %copy-done.2, f32[3,2,8,128]{3,1,2,0:T(2,128)} %collective-permute-done.18, f32[6,16,14,3]{3,1,2,0:T(8,128)S(1)} %copy.115, ...), kind=kLoop, calls=%fused_computation.73 | loop fusion | flops 2654208 | bytes 2735616 | tf_op jit(solution)/shard_map/add | solution.py:166
  129.1 0.7 copy.117
  (132 shorter events, 17.3 us)
Async XLA Ops:
  0.0 22.0 %copy-start = (f32[16,16]{1,0:T(8,128)S(1)}, f32[16,16]{1,0:T(8,128)}, u32[]{:S(2)}) copy-start(f32[16,16]{1,0:T(8,128)} %param.11) | copy-start | bytes 3076
  0.0 11.4 %copy-start.13 = (s32[8]{0:T(128)S(1)}, s32[8]{0:T(128)}, u32[]{:S(2)}) copy-start(s32[8]{0:T(128)} %param.15) | copy-start | bytes 100
  1.0 10.8 %copy-start.16 = (s32[8]{0:T(128)S(1)}, s32[8]{0:T(128)}, u32[]{:S(2)}) copy-start(s32[8]{0:T(128)} %param.16) | copy-start | bytes 100
  1.0 11.0 %copy-start.4 = (f32[4,1,1,16,16]{4,3,2,1,0:T(8,128)S(1)}, f32[4,1,1,16,16]{4,3,2,1,0:T(8,128)}, u32[]{:S(2)}) copy-start(f32[4,1,1,16,16]{4,3,2,1,0:T(8,128)} %param.17) | copy-start | bytes 12292
  1.0 16.6 %collective-permute-start.3 = (f32[3,16,3,128]{3,1,2,0:T(8,128)S(1)}, f32[3,16,3,128]{3,1,2,0:T(8,128)S(1)}, u32[]{:S(2)}, u32[]{:S(2)}) collective-permute-start(f32[3,16,3,128]{3,1,2,0:T(8,128)S(1)} %get-tuple-element.52), channel_id=1, source_target_pairs={{0,4},{4,8},{8,12},{12,0},{1,5},{5,9},{9,13},{13,1},{2,6},{6,10},{... | collective-permute-start | bytes 221192 | tf_op jit(solution)/shard_map/ppermute | solution.py:21
  1.6 16.2 %collective-permute-start.2 = (f32[3,16,3,128]{3,1,2,0:T(8,128)S(1)}, f32[3,16,3,128]{3,1,2,0:T(8,128)S(1)}, u32[]{:S(2)}, u32[]{:S(2)}) collective-permute-start(f32[3,16,3,128]{3,1,2,0:T(8,128)S(1)} %get-tuple-element.51), channel_id=1, source_target_pairs={{4,0},{8,4},{12,8},{0,12},{5,1},{9,5},{13,9},{1,13},{6,2},{10,6},{... | collective-permute-start | bytes 221192 | tf_op jit(solution)/shard_map/ppermute | solution.py:23
  3.6 18.3 %collective-permute-start.1 = (f32[3,2,8,128]{3,1,2,0:T(2,128)S(1)}, f32[3,2,8,128]{3,1,2,0:T(2,128)S(1)}, u32[]{:S(2)}, u32[]{:S(2)}) collective-permute-start(f32[3,2,8,128]{3,1,2,0:T(2,128)S(1)} %get-tuple-element.44), channel_id=1, source_target_pairs={{0,16},{1,17},{2,18},{3,19},{4,20},{5,21},{6,22},{7,23},{8,24},{9,... | collective-permute-start | bytes 73736 | tf_op jit(solution)/shard_map/ppermute | solution.py:21
  7.8 14.1 %collective-permute-start = (f32[3,2,8,128]{3,1,2,0:T(2,128)S(1)}, f32[3,2,8,128]{3,1,2,0:T(2,128)S(1)}, u32[]{:S(2)}, u32[]{:S(2)}) collective-permute-start(f32[3,2,8,128]{3,1,2,0:T(2,128)S(1)} %get-tuple-element.43), channel_id=1, source_target_pairs={{16,0},{17,1},{18,2},{19,3},{20,4},{21,5},{22,6},{23,7},{24,8},{25... | collective-permute-start | bytes 73736 | tf_op jit(solution)/shard_map/ppermute | solution.py:23
  10.0 7.6 %copy-start.1 = (f32[3,16,8,128]{3,2,1,0:T(8,128)S(1)}, f32[3,16,8,128]{3,2,1,0:T(8,128)}, u32[]{:S(2)}) copy-start(f32[3,16,8,128]{3,2,1,0:T(8,128)} %param.9) | copy-start | bytes 589828
  11.8 60.3 %copy-start.11 = (pred[8]{0:T(512)(128)(4,1)}, pred[8]{0:T(512)(128)(4,1)S(1)}, u32[]{:S(2)}) copy-start(pred[8]{0:T(512)(128)(4,1)S(1)} %broadcast_compare_fusion.1) | copy-start | bytes 28
  17.6 54.4 %copy-start.9 = (s32[8]{0:T(128)}, s32[8]{0:T(128)S(1)}, u32[]{:S(2)}) copy-start(s32[8]{0:T(128)S(1)} %select_reduce_fusion) | copy-start | bytes 100
  17.7 4.6 %copy-start.7 = (f32[2,16]{1,0:T(2,128)S(1)}, f32[2,16]{1,0:T(2,128)}, u32[]{:S(2)}) copy-start(f32[2,16]{1,0:T(2,128)} %param.12) | copy-start | bytes 388
  17.8 9.3 %copy-start.5 = (f32[4,4]{1,0:T(4,128)S(1)}, f32[4,4]{1,0:T(4,128)}, u32[]{:S(2)}) copy-start(f32[4,4]{1,0:T(4,128)} %param.14) | copy-start | bytes 196
  17.8 17.3 %copy-start.6 = (f32[16,2]{0,1:T(2,128)S(1)}, f32[16,2]{0,1:T(2,128)}, u32[]{:S(2)}) copy-start(f32[16,2]{0,1:T(2,128)} %param.13) | copy-start | bytes 388
  18.0 12.8 %collective-permute-start.5 = (f32[3,16,14,3]{3,1,2,0:T(8,128)S(1)}, f32[3,16,14,3]{3,1,2,0:T(8,128)S(1)}, u32[]{:S(2)}, u32[]{:S(2)}) collective-permute-start(f32[3,16,14,3]{3,1,2,0:T(8,128)S(1)} %get-tuple-element.20), channel_id=1, source_target_pairs={{0,1},{1,2},{2,3},{3,0},{4,5},{5,6},{6,7},{7,4},{8,9},{9,10},{10,1... | collective-permute-start | bytes 24200 | tf_op jit(solution)/shard_map/ppermute | solution.py:21
  19.6 15.5 %collective-permute-start.4 = (f32[3,16,14,3]{3,1,2,0:T(8,128)S(1)}, f32[3,16,14,3]{3,1,2,0:T(8,128)S(1)}, u32[]{:S(2)}, u32[]{:S(2)}) collective-permute-start(f32[3,16,14,3]{3,1,2,0:T(8,128)S(1)} %get-tuple-element.19), channel_id=1, source_target_pairs={{1,0},{2,1},{3,2},{0,3},{5,4},{6,5},{7,6},{4,7},{9,8},{10,9},{11,1... | collective-permute-start | bytes 24200 | tf_op jit(solution)/shard_map/ppermute | solution.py:23
  37.0 8.8 %collective-permute-start.7 = (f32[3,2,8,128]{3,1,2,0:T(2,128)S(1)}, f32[3,2,8,128]{3,1,2,0:T(2,128)S(1)}, u32[]{:S(2)}, u32[]{:S(2)}) collective-permute-start(f32[3,2,8,128]{3,1,2,0:T(2,128)S(1)} %get-tuple-element.42), channel_id=1, source_target_pairs={{0,16},{1,17},{2,18},{3,19},{4,20},{5,21},{6,22},{7,23},{8,24},{9,... | collective-permute-start | bytes 73736 | tf_op jit(solution)/shard_map/ppermute | solution.py:21
  40.7 5.7 %collective-permute-start.6 = (f32[3,2,8,128]{3,1,2,0:T(2,128)S(1)}, f32[3,2,8,128]{3,1,2,0:T(2,128)S(1)}, u32[]{:S(2)}, u32[]{:S(2)}) collective-permute-start(f32[3,2,8,128]{3,1,2,0:T(2,128)S(1)} %get-tuple-element.41), channel_id=1, source_target_pairs={{16,0},{17,1},{18,2},{19,3},{20,4},{21,5},{22,6},{23,7},{24,8},{25... | collective-permute-start | bytes 73736 | tf_op jit(solution)/shard_map/ppermute | solution.py:23
  44.0 7.8 %collective-permute-start.9 = (f32[3,16,3,128]{3,1,2,0:T(8,128)S(1)}, f32[3,16,3,128]{3,1,2,0:T(8,128)S(1)}, u32[]{:S(2)}, u32[]{:S(2)}) collective-permute-start(f32[3,16,3,128]{3,1,2,0:T(8,128)S(1)} %get-tuple-element.38), channel_id=1, source_target_pairs={{0,4},{4,8},{8,12},{12,0},{1,5},{5,9},{9,13},{13,1},{2,6},{6,10},{... | collective-permute-start | bytes 221192 | tf_op jit(solution)/shard_map/ppermute | solution.py:21
  44.1 7.8 %collective-permute-start.8 = (f32[3,16,3,128]{3,1,2,0:T(8,128)S(1)}, f32[3,16,3,128]{3,1,2,0:T(8,128)S(1)}, u32[]{:S(2)}, u32[]{:S(2)}) collective-permute-start(f32[3,16,3,128]{3,1,2,0:T(8,128)S(1)} %get-tuple-element.37), channel_id=1, source_target_pairs={{4,0},{8,4},{12,8},{0,12},{5,1},{9,5},{13,9},{1,13},{6,2},{10,6},{... | collective-permute-start | bytes 221192 | tf_op jit(solution)/shard_map/ppermute | solution.py:23
  52.1 12.8 %collective-permute-start.11 = (f32[3,16,14,3]{3,1,2,0:T(8,128)S(1)}, f32[3,16,14,3]{3,1,2,0:T(8,128)S(1)}, u32[]{:S(2)}, u32[]{:S(2)}) collective-permute-start(f32[3,16,14,3]{3,1,2,0:T(8,128)S(1)} %get-tuple-element.18), channel_id=1, source_target_pairs={{0,1},{1,2},{2,3},{3,0},{4,5},{5,6},{6,7},{7,4},{8,9},{9,10},{10,1... | collective-permute-start | bytes 24200 | tf_op jit(solution)/shard_map/ppermute | solution.py:21
  53.3 15.1 %collective-permute-start.10 = (f32[3,16,14,3]{3,1,2,0:T(8,128)S(1)}, f32[3,16,14,3]{3,1,2,0:T(8,128)S(1)}, u32[]{:S(2)}, u32[]{:S(2)}) collective-permute-start(f32[3,16,14,3]{3,1,2,0:T(8,128)S(1)} %get-tuple-element.17), channel_id=1, source_target_pairs={{1,0},{2,1},{3,2},{0,3},{5,4},{6,5},{7,6},{4,7},{9,8},{10,9},{11,1... | collective-permute-start | bytes 24200 | tf_op jit(solution)/shard_map/ppermute | solution.py:23
  73.1 10.8 %collective-permute-start.14 = (f32[6,16,3,128]{3,1,2,0:T(8,128)S(1)}, f32[6,16,3,128]{3,1,2,0:T(8,128)S(1)}, u32[]{:S(2)}, u32[]{:S(2)}) collective-permute-start(f32[6,16,3,128]{3,1,2,0:T(8,128)S(1)} %get-tuple-element.16), channel_id=1, source_target_pairs={{4,0},{8,4},{12,8},{0,12},{5,1},{9,5},{13,9},{1,13},{6,2},{10,6},{... | collective-permute-start | bytes 442376 | tf_op jit(solution)/shard_map/ppermute | solution.py:23
  73.3 10.6 %collective-permute-start.15 = (f32[6,16,3,128]{3,1,2,0:T(8,128)S(1)}, f32[6,16,3,128]{3,1,2,0:T(8,128)S(1)}, u32[]{:S(2)}, u32[]{:S(2)}) collective-permute-start(f32[6,16,3,128]{3,1,2,0:T(8,128)S(1)} %get-tuple-element.15), channel_id=1, source_target_pairs={{0,4},{4,8},{8,12},{12,0},{1,5},{5,9},{9,13},{13,1},{2,6},{6,10},{... | collective-permute-start | bytes 442376 | tf_op jit(solution)/shard_map/ppermute | solution.py:21
  79.0 18.2 %collective-permute-start.13 = (f32[3,2,8,128]{3,1,2,0:T(2,128)S(1)}, f32[3,2,8,128]{3,1,2,0:T(2,128)S(1)}, u32[]{:S(2)}, u32[]{:S(2)}) collective-permute-start(f32[3,2,8,128]{3,1,2,0:T(2,128)S(1)} %get-tuple-element.34), channel_id=1, source_target_pairs={{0,16},{1,17},{2,18},{3,19},{4,20},{5,21},{6,22},{7,23},{8,24},{9,... | collective-permute-start | bytes 73736 | tf_op jit(solution)/shard_map/ppermute | solution.py:21
  82.6 14.5 %collective-permute-start.12 = (f32[3,2,8,128]{3,1,2,0:T(2,128)S(1)}, f32[3,2,8,128]{3,1,2,0:T(2,128)S(1)}, u32[]{:S(2)}, u32[]{:S(2)}) collective-permute-start(f32[3,2,8,128]{3,1,2,0:T(2,128)S(1)} %get-tuple-element.33), channel_id=1, source_target_pairs={{16,0},{17,1},{18,2},{19,3},{20,4},{21,5},{22,6},{23,7},{24,8},{25... | collective-permute-start | bytes 73736 | tf_op jit(solution)/shard_map/ppermute | solution.py:23
  85.0 8.8 %collective-permute-start.17 = (f32[6,16,14,3]{2,1,3,0:T(8,128)S(1)}, f32[6,16,14,3]{2,1,3,0:T(8,128)S(1)}, u32[]{:S(2)}, u32[]{:S(2)}) collective-permute-start(f32[6,16,14,3]{2,1,3,0:T(8,128)S(1)} %copy.102), channel_id=1, source_target_pairs={{0,1},{1,2},{2,3},{3,0},{4,5},{5,6},{6,7},{7,4},{8,9},{9,10},{10,1... | collective-permute-start | bytes 48392 | tf_op jit(solution)/shard_map/ppermute | solution.py:21
  86.7 11.1 %copy-start.3 = (f32[16,8,128]{2,0,1:T(8,128)S(1)}, f32[16,8,128]{2,0,1:T(8,128)}, u32[]{:S(2)}) copy-start(f32[16,8,128]{2,0,1:T(8,128)} %copy.110) | copy-start | bytes 196612
  86.7 11.1 %copy-start.10 = (s32[8]{0:T(128)S(1)}, s32[8]{0:T(128)}, u32[]{:S(2)}) copy-start(s32[8]{0:T(128)} %copy-done.9) | copy-start | bytes 100
  86.7 11.1 %copy-start.12 = (pred[8]{0:T(512)(128)(4,1)S(1)}, pred[8]{0:T(512)(128)(4,1)}, u32[]{:S(2)}) copy-start(pred[8]{0:T(512)(128)(4,1)} %copy-done.11) | copy-start | bytes 28
  86.7 8.8 %collective-permute-start.16 = (f32[6,16,14,3]{2,1,3,0:T(8,128)S(1)}, f32[6,16,14,3]{2,1,3,0:T(8,128)}, u32[]{:S(2)}, u32[]{:S(2)}) collective-permute-start(f32[6,16,14,3]{2,1,3,0:T(8,128)S(1)} %copy.100), channel_id=1, source_target_pairs={{1,0},{2,1},{3,2},{0,3},{5,4},{6,5},{7,6},{4,7},{9,8},{10,9},{11,1... | collective-permute-start | bytes 48392 | tf_op jit(solution)/shard_map/ppermute | solution.py:23
  97.2 0.6 copy-start.14
  97.2 0.6 copy-start.15
  100.0 6.4 %copy-start.8 = (f32[2,16]{1,0:T(2,128)S(1)}, f32[2,16]{1,0:T(2,128)}, u32[]{:S(2)}) copy-start(f32[2,16]{1,0:T(2,128)} %param.12) | copy-start | bytes 388
  105.8 7.4 %collective-permute-start.20 = (f32[6,16,3,128]{3,1,2,0:T(8,128)S(1)}, f32[6,16,3,128]{3,1,2,0:T(8,128)S(1)}, u32[]{:S(2)}, u32[]{:S(2)}) collective-permute-start(f32[6,16,3,128]{3,1,2,0:T(8,128)S(1)} %get-tuple-element.12), channel_id=1, source_target_pairs={{4,0},{8,4},{12,8},{0,12},{5,1},{9,5},{13,9},{1,13},{6,2},{10,6},{... | collective-permute-start | bytes 442376 | tf_op jit(solution)/shard_map/ppermute | solution.py:23
  105.8 7.4 %collective-permute-start.21 = (f32[6,16,3,128]{3,1,2,0:T(8,128)S(1)}, f32[6,16,3,128]{3,1,2,0:T(8,128)S(1)}, u32[]{:S(2)}, u32[]{:S(2)}) collective-permute-start(f32[6,16,3,128]{3,1,2,0:T(8,128)S(1)} %get-tuple-element.11), channel_id=1, source_target_pairs={{0,4},{4,8},{8,12},{12,0},{1,5},{5,9},{9,13},{13,1},{2,6},{6,10},{... | collective-permute-start | bytes 442376 | tf_op jit(solution)/shard_map/ppermute | solution.py:21
  106.7 10.1 %copy-start.2 = (f32[3,16,8,128]{3,1,2,0:T(8,128)}, f32[3,16,8,128]{3,1,2,0:T(8,128)S(1)}, u32[]{:S(2)}) copy-start(f32[3,16,8,128]{3,1,2,0:T(8,128)S(1)} %fusion.5) | copy-start | bytes 589828
  107.4 19.8 %collective-permute-start.19 = (f32[3,2,8,128]{3,1,2,0:T(2,128)}, f32[3,2,8,128]{3,1,2,0:T(2,128)}, u32[]{:S(2)}, u32[]{:S(2)}) collective-permute-start(f32[3,2,8,128]{3,1,2,0:T(2,128)} %get-tuple-element.27), channel_id=1, source_target_pairs={{0,16},{1,17},{2,18},{3,19},{4,20},{5,21},{6,22},{7,23},{8,24},{9,... | collective-permute-start | bytes 73736 | tf_op jit(solution)/shard_map/ppermute | solution.py:21
  111.9 15.3 %collective-permute-start.18 = (f32[3,2,8,128]{3,1,2,0:T(2,128)}, f32[3,2,8,128]{3,1,2,0:T(2,128)}, u32[]{:S(2)}, u32[]{:S(2)}) collective-permute-start(f32[3,2,8,128]{3,1,2,0:T(2,128)} %get-tuple-element.26), channel_id=1, source_target_pairs={{16,0},{17,1},{18,2},{19,3},{20,4},{21,5},{22,6},{23,7},{24,8},{25... | collective-permute-start | bytes 73736 | tf_op jit(solution)/shard_map/ppermute | solution.py:23
  115.0 8.8 %collective-permute-start.23 = (f32[6,16,14,3]{2,1,3,0:T(8,128)}, f32[6,16,14,3]{2,1,3,0:T(8,128)S(1)}, u32[]{:S(2)}, u32[]{:S(2)}) collective-permute-start(f32[6,16,14,3]{2,1,3,0:T(8,128)} %copy.114), channel_id=1, source_target_pairs={{0,1},{1,2},{2,3},{3,0},{4,5},{5,6},{6,7},{7,4},{8,9},{9,10},{10,1... | collective-permute-start | bytes 48392 | tf_op jit(solution)/shard_map/ppermute | solution.py:21
  116.8 8.7 %collective-permute-start.22 = (f32[6,16,14,3]{2,1,3,0:T(8,128)S(1)}, f32[6,16,14,3]{2,1,3,0:T(8,128)}, u32[]{:S(2)}, u32[]{:S(2)}) collective-permute-start(f32[6,16,14,3]{2,1,3,0:T(8,128)S(1)} %copy.112), channel_id=1, source_target_pairs={{1,0},{2,1},{3,2},{0,3},{5,4},{6,5},{7,6},{4,7},{9,8},{10,9},{11,1... | collective-permute-start | bytes 48392 | tf_op jit(solution)/shard_map/ppermute | solution.py:23
where the time goes:
time: 130 us
  starting transfers between devices  42.3 us (33%)
  waiting for transfers between devices  29.4 us (23%)
  blocking collectives  23.5 us (18%)
  local copies, waits for them, and re-layouts  18.1 us (14%)
  matrix products  9.75 us (8%)
  other arithmetic  5.91 us (5%)
    ppermute x12, starting transfers between devices, extended(): lax.ppermute(tail, axis, [(i, (i + 1) % count) for i in range(ends)])  22.3 us
    ppermute x12, starting transfers between devices, extended(): lax.ppermute(head, axis, [((i + 1) % count, i) for i in range(ends)])  20 us
    ppermute x12, waiting for transfers between devices, extended(): lax.ppermute(tail, axis, [(i, (i + 1) % count) for i in range(ends)])  19 us
    all_gather x4, blocking collectives, interface_sum(): lax.all_gather(edge_values, 'gx', axis=0, tiled=True)  18.4 us
    ppermute x12, waiting for transfers between devices, extended(): lax.ppermute(head, axis, [((i + 1) % count, i) for i in range(ends)])  10.4 us
    all_gather x1, blocking collectives, local(): every_inv = lax.all_gather(inverse_here, 'gx', axis=0, tiled=True)  5.17 us
    ppermute x2, local copies, waits for them, and re-layouts, extended(): lax.ppermute(head, axis, [((i + 1) % count, i) for i in range(ends)])  3.3 us
    slice x12, local copies, waits for them, and re-layouts, extended(): head = lax.slice_in_dim(cells, 0, width, axis=dim)  3.04 us
  transfers between devices with their start and end apart: 24, of which 9 were waited for; matrix products, arithmetic and copies ran while one was open for 15% of the time, Pallas kernels for 0%

commit v1 on v0

v1 whole, which is shorter than its diff:
```python
import functools

import jax
import jax.numpy as jnp
from jax import lax
from jax.experimental import pallas as pl
from jax.experimental.pallas import tpu as pltpu
from jax.sharding import PartitionSpec as P

WIN = 8
time_step = 0.15
NEAR = 7.0 / 9.0
FAR = 1.0 / 36.0
C1 = 45.0 / 60.0
C2 = -9.0 / 60.0
C3 = 1.0 / 60.0
MESH = pl.DeviceIdType.MESH
high = lax.Precision.HIGHEST


def weighted(terms):
    chains = [None, None]
    for n, (coef, block) in enumerate(terms):
        part = coef * block
        chains[n % 2] = part if chains[n % 2] is None else chains[n % 2] + part
    return chains[0] if chains[1] is None else chains[0] + chains[1]


def kernel(
    sizes,
    dir_ref, base_ref, inv_ref,
    local_s, in_s, out_s, schur_s, plane_s, slot_s,
    res_ref,
    state_one, state_two, force, acc, rhs, obs, prod_y, prod_z, hbuf,
    yside, xrecv, ysend, yrecv, zsend, zrecv, edge, winrecv, lanes_inv, blocks,
    xs_sem, xr_sem, ys_sem, yr_sem, zs_sem, zr_sem, es_sem, er_sem, ws_sem, wr_sem,
):
    n_gx, n_gy, n_gz = sizes
    gx, gy, gz = lax.axis_index("gx"), lax.axis_index("gy"), lax.axis_index("gz")
    comps, cx, cy, cz = dir_ref.shape
    half = ysend.shape[4]
    owned = inv_ref.shape[0]
    y_next, y_prev = lax.rem(gy + 1, n_gy), lax.rem(gy + n_gy - 1, n_gy)
    z_next, z_prev = lax.rem(gz + 1, n_gz), lax.rem(gz + n_gz - 1, n_gz)

    @pl.when(gx == 0)
    def _():
        xrecv[:, 0] = jnp.zeros(xrecv.shape[:1] + xrecv.shape[2:], jnp.float32)

    @pl.when(gx == n_gx - 1)
    def _():
        xrecv[:, 1] = jnp.zeros(xrecv.shape[:1] + xrecv.shape[2:], jnp.float32)

    barrier = pltpu.get_barrier_semaphore()
    for d in range(1, n_gx):
        pl.semaphore_signal(barrier, device_id={"gx": lax.rem(gx + d, n_gx)}, device_id_type=MESH)
    for q in (y_prev, y_next):
        pl.semaphore_signal(barrier, device_id={"gy": q}, device_id_type=MESH)
    for q in (z_prev, z_next):
        pl.semaphore_signal(barrier, device_id={"gz": q}, device_id_type=MESH)

    def remote(src, dst, send, recv, where):
        return pltpu.make_async_remote_copy(
            src_ref=src, dst_ref=dst, send_sem=send, recv_sem=recv,
            device_id=where, device_id_type=MESH,
        )

    lane = lax.broadcasted_iota(jnp.int32, (comps, cy, cz), 2)
    sub = lax.broadcasted_iota(jnp.int32, (comps, cy, cz), 1)
    in_group = lane % WIN

    def x_copies(r, src):
        right = remote(src.at[:, cx - 2 : cx], xrecv.at[r, 0], xs_sem.at[r, 0], xr_sem.at[r, 0],
                       {"gx": lax.rem(gx + 1, n_gx)})
        left = remote(src.at[:, 0:2], xrecv.at[r, 1], xs_sem.at[r, 1], xr_sem.at[r, 1],
                      {"gx": lax.rem(gx + n_gx - 1, n_gx)})
        return right, left

    def x_start(copies):
        right, left = copies

        @pl.when(gx < n_gx - 1)
        def _():
            right.start()

        @pl.when(gx > 0)
        def _():
            left.start()

    def x_arrived(copies):
        right, left = copies

        @pl.when(gx > 0)
        def _():
            right.wait_recv()

        @pl.when(gx < n_gx - 1)
        def _():
            left.wait_recv()

    def x_sent(copies):
        right, left = copies

        @pl.when(gx < n_gx - 1)
        def _():
            right.wait_send()

        @pl.when(gx > 0)
        def _():
            left.wait_send()

    def y_copies(r):
        return (
            remote(ysend.at[r, 0], yrecv.at[r, 0], ys_sem.at[r, 0], yr_sem.at[r, 0], {"gy": y_prev}),
            remote(ysend.at[r, 1], yrecv.at[r, 1], ys_sem.at[r, 1], yr_sem.at[r, 1], {"gy": y_next}),
        )

    def z_copies(r):
        return (
            remote(zsend.at[r], zrecv.at[r, 0], zs_sem.at[r, 0], zr_sem.at[r, 0], {"gz": z_prev}),
            remote(zsend.at[r], zrecv.at[r, 1], zs_sem.at[r, 1], zr_sem.at[r, 1], {"gz": z_next}),
        )

    def edge_copies(r):
        return tuple(
            remote(edge.at[r, 0], edge.at[r, d], es_sem.at[r, d], er_sem.at[r, d],
                   {"gx": lax.rem(gx + d, n_gx)})
            for d in range(1, n_gx)
        )

    win_copies = tuple(
        remote(inv_ref, winrecv.at[d - 1], ws_sem.at[d], wr_sem.at[d], {"gx": lax.rem(gx + d, n_gx)})
        for d in range(1, n_gx)
    )

    def start(copies):
        for copy in copies:
            copy.start()

    def arrived(copies):
        for copy in copies:
            copy.wait_recv()

    def pack_y(r, src):
        ysend[r, 0] = src[:, :, 0:half, :]
        ysend[r, 1] = src[:, :, cy - half : cy, :]

    def pack_z(r, src):
        packed = None
        for i in range(cx):
            block = src[:, i]
            turned = block if i == 0 else pltpu.roll(block, WIN * i, 2)
            if packed is None:
                packed = turned
            else:
                packed = jnp.where((lane >= WIN * i - 4) & (lane < WIN * i + 4), turned, packed)
        zsend[r] = packed

    def circular_z(block):
        def diff(k):
            return pltpu.roll(block, cz - k, 2) - pltpu.roll(block, k, 2)

        return C1 * diff(1) + C2 * diff(2) + C3 * diff(3)

    def z_fix(r):
        true = jnp.where(in_group < 4, zrecv[r, 0], zrecv[r, 1])
        delta = true - zsend[r]
        low = jnp.where(in_group >= WIN - 3, delta, 0.0)
        top = jnp.where(in_group < 3, delta, 0.0)
        low_fix = -(C1 * pltpu.roll(low, 1, 2) + C2 * pltpu.roll(low, 2, 2) + C3 * pltpu.roll(low, 3, 2))
        top_fix = (C1 * pltpu.roll(top, cz - 1, 2) + C2 * pltpu.roll(top, cz - 2, 2)
                   + C3 * pltpu.roll(top, cz - 3, 2))
        return jnp.where(in_group < 3, low_fix, 0.0) + jnp.where(in_group >= WIN - 3, top_fix, 0.0)

    def z_fix_of(fix, i):
        turned = fix if i == 0 else pltpu.roll(fix, (cz - WIN * i) % cz, 2)
        return jnp.where((lane < 3) | (lane >= cz - 3), turned, 0.0)

    def fill_sides(r):
        yside[:, :, 0:half, :] = yrecv[r, 0]
        yside[:, :, cy - half : cy, :] = yrecv[r, 1]

    def along_y(block, side):
        def diff(k):
            ahead = pltpu.roll(jnp.where(sub < k, side, block), cy - k, 1)
            behind = pltpu.roll(jnp.where(sub >= cy - k, side, block), k, 1)
            return ahead - behind

        return C1 * diff(1) + C2 * diff(2) + C3 * diff(3)

    def stencil_x(src, r, i):
        def row(n):
            if n < 0:
                return xrecv[r, 0, :, n + 2]
            if n >= cx:
                return xrecv[r, 1, :, n - cx]
            return src[:, n]

        return NEAR * (row(i + 1) - row(i - 1)) + FAR * (row(i + 2) - row(i - 2))

    def velocity(n, c, i):
        return base_ref[n, c, i].astype(jnp.float32)[None]

    def fold(blocks8):
        level, m = list(blocks8), 1
        while len(level) > 1:
            keep = (lane & m) == 0
            level = [
                jnp.where(keep, a + pltpu.roll(a, cz - m, 2), b + pltpu.roll(b, m, 2))
                for a, b in zip(level[0::2], level[1::2])
            ]
            m *= 2
        return level[0]

    def unfold(block):
        level, m = [block], WIN // 2
        while m >= 1:
            keep = (lane & m) == 0
            wider = []
            for t in level:
                wider.append(jnp.where(keep, t, pltpu.roll(t, m, 2)))
                wider.append(jnp.where(keep, pltpu.roll(t, cz - m, 2), t))
            level = wider
            m //= 2
        return level

    def observe(src, dst):
        for g in range(cx // WIN):
            sums = fold([src[:, g * WIN + k] for k in range(WIN)])
            mixed = lax.dot_general(
                sums.reshape(comps * cy, cz), blocks[g], (((1,), (1,)), ((), ())),
                precision=high, preferred_element_type=jnp.float32,
            ).reshape(comps, cy, cz)
            for k, t in enumerate(unfold(mixed)):
                dst[:, g * WIN + k] = t

    def build_blocks():
        count = inv_ref.shape[2]
        spread = (
            lax.broadcasted_iota(jnp.int32, (count, cz), 1) // WIN
            == lax.broadcasted_iota(jnp.int32, (count, cz), 0)
        ).astype(jnp.float32)
        for d in range(n_gx):
            source = inv_ref[...] if d == 0 else winrecv[d - 1]
            lanes_inv[d * owned : (d + 1) * owned] = jnp.dot(
                source.reshape(owned * count, count), spread,
                precision=high, preferred_element_type=jnp.float32,
            ).reshape(owned, count, cz) * (1.0 / (WIN * WIN))
        blocks[...] = jnp.zeros(blocks.shape, jnp.float32)
        row = lax.broadcasted_iota(jnp.int32, (WIN, cz), 0)
        col = lax.broadcasted_iota(jnp.int32, (WIN, cz), 1) % WIN

        def add_slot(j, carry):
            owner = lax.rem(gx + n_gx - j // owned, n_gx)
            cell = plane_s[slot_s[owner * owned + j % owned]] - gx * cx
            for g in range(cx // WIN):
                here = (row == cell - g * WIN) & (col == cell - g * WIN)
                for s in range(count):
                    line = jnp.broadcast_to(lanes_inv[j, s : s + 1, :], (WIN, cz))
                    blocks[g, s * WIN : (s + 1) * WIN, :] += jnp.where(here, line, 0.0)
            return carry

        lax.fori_loop(0, n_gx * owned, add_slot, 0)

    def interface(r, m, transposed):
        terms = []
        for d in range(n_gx):
            owner = lax.rem(gx + n_gx - d, n_gx)
            for k in range(2):
                n, own = 2 * owner + k, 2 * gx + m
                coef = schur_s[n, own] if transposed else schur_s[own, n]
                terms.append((coef, edge[r, d, k]))
        return weighted(terms)

    sent = []

    def tangent(r, n, src, dst, first, shadow):
        xc, yc, zc, ec = x_copies(r, src), y_copies(r), z_copies(r), edge_copies(r)
        if not first:
            x_start(xc)
        pack_z(r, src)
        if not first:
            start(zc)
        pack_y(r, src)
        if first:
            pl.semaphore_wait(barrier, n_gx - 1 + 4)
            x_start(xc)
            start(zc)
        start(yc)
        sent.append((xc, yc + zc + ec))
        for i in range(cx):
            block = src[:, i]
            acc[:, i] = block - time_step * (velocity(n, 2, i) * circular_z(block))
        x_arrived(xc)
        for i in range(cx):
            rhs[:, i] = stencil_x(src, r, i)
        for k in range(2):
            edge[r, 0, k] = weighted([(in_s[k, j], rhs[:, j]) for j in range(cx)])
        start(ec)
        if first:
            start(win_copies)
        for i in range(cx):
            solved = weighted([(local_s[i, j], rhs[:, j]) for j in range(cx)])
            acc[:, i] -= time_step * (velocity(n, 0, i) * solved)
        shadow()
        arrived(yc)
        fill_sides(r)
        for i in range(cx):
            acc[:, i] -= time_step * (velocity(n, 1, i) * along_y(src[:, i], yside[:, i]))
        arrived(zc)
        fix = z_fix(r)
        arrived(ec)
        values = [interface(r, m, False) for m in range(2)]
        for i in range(cx):
            pulled = out_s[i, 0] * values[0] + out_s[i, 1] * values[1]
            dst[:, i] = acc[:, i] - time_step * (
                velocity(n, 0, i) * pulled + velocity(n, 2, i) * z_fix_of(fix, i)
            )

    def adjoint(r, n, src, dst, extra):
        xc, yc, zc, ec = x_copies(r, hbuf.at[r - 2]), y_copies(r), z_copies(r), edge_copies(r)
        sent.append((xc, yc + zc + ec))
        held = hbuf.at[r - 2]
        for i in range(cx):
            block = src[:, i]
            rhs[:, i] = velocity(n, 0, i) * block
            prod_y[:, i] = velocity(n, 1, i) * block
            prod_z[:, i] = velocity(n, 2, i) * block
        for k in range(2):
            edge[r, 0, k] = weighted([(out_s[i, k], rhs[:, i]) for i in range(cx)])
        start(ec)
        pack_z(r, prod_z)
        start(zc)
        pack_y(r, prod_y)
        start(yc)
        order = (0, 1, cx - 2, cx - 1) + tuple(range(2, cx - 2))
        for i in order:
            acc[:, i] = weighted([(local_s[j, i], rhs[:, j]) for j in range(cx)])
        arrived(ec)
        values = [interface(r, m, True) for m in range(2)]
        for place, i in enumerate(order):
            held[:, i] = acc[:, i] + (in_s[0, i] * values[0] + in_s[1, i] * values[1])
            if place == 3:
                x_start(xc)
        for i in range(cx):
            total = src[:, i] + time_step * circular_z(prod_z[:, i])
            acc[:, i] = total if extra is None else total + extra[:, i]
        for i in range(2, cx - 2):
            acc[:, i] += time_step * stencil_x(held, r, i)
        arrived(yc)
        fill_sides(r)
        for i in range(cx):
            acc[:, i] += time_step * along_y(prod_y[:, i], yside[:, i])
        arrived(zc)
        fix = z_fix(r)
        x_arrived(xc)
        for i in range(cx):
            total = acc[:, i] + time_step * z_fix_of(fix, i)
            if i < 2 or i >= cx - 2:
                total = total + time_step * stencil_x(held, r, i)
            dst[:, i] = total

    def nothing():
        pass

    def observe_one():
        arrived(win_copies)
        build_blocks()
        observe(state_one, obs)

    tangent(0, 0, dir_ref, state_one, True, nothing)
    tangent(1, 1, state_one, state_two, False, observe_one)
    observe(state_two, force)
    adjoint(2, 1, force, state_two, obs)
    adjoint(3, 0, state_two, res_ref, None)
    for xc, rest in sent:
        x_sent(xc)
        for copy in rest:
            copy.wait_send()
    for copy in win_copies:
        copy.wait_send()


def solution(mesh):
    sizes = tuple(mesh.shape[name] for name in ("gx", "gy", "gz"))

    def local(direction, base_flow, local_inv, couple_in, couple_out, schur_inv,
              plane_x, slot_plane, window_inv):
        n_gx = sizes[0]
        comps, cx, cy, cz = direction.shape
        owned, count = window_inv.shape[0], window_inv.shape[3]
        half = max(3, cy // 2)
        field = pltpu.VMEM(direction.shape, jnp.float32)

        def held(*shape):
            return pltpu.VMEM(shape, jnp.float32)

        sems = pltpu.SemaphoreType.DMA
        vmem = pl.BlockSpec(memory_space=pltpu.VMEM)
        smem = pl.BlockSpec(memory_space=pltpu.SMEM)
        pulled = pl.pallas_call(
            functools.partial(kernel, sizes),
            out_shape=jax.ShapeDtypeStruct(direction.shape, jnp.float32),
            in_specs=[vmem] * 3 + [smem] * 6,
            out_specs=vmem,
            scratch_shapes=[field] * 8 + [
                held(2, comps, cx, cy, cz),
                field,
                held(4, 2, comps, 2, cy, cz),
                held(4, 2, comps, cx, half, cz),
                held(4, 2, comps, cx, half, cz),
                held(4, comps, cy, cz),
                held(4, 2, comps, cy, cz),
                held(4, n_gx, 2, comps, cy, cz),
                held(n_gx - 1, owned, count, count),
                held(n_gx * owned, count, cz),
                held(cx // WIN, count * WIN, cz),
                sems((4, 2)), sems((4, 2)), sems((4, 2)), sems((4, 2)), sems((4, 2)), sems((4, 2)),
                sems((4, n_gx)), sems((4, n_gx)), sems((n_gx,)), sems((n_gx,)),
            ],
            compiler_params=pltpu.CompilerParams(collective_id=0, has_side_effects=True),
        )(
            direction, base_flow, window_inv.reshape(owned, count, count),
            local_inv, couple_in, couple_out, schur_inv, plane_x, slot_plane,
        )
        return pulled + direction

    return jax.shard_map(
        local,
        mesh=mesh,
        in_specs=(
            P(None, "gx", "gy", "gz"),
            P(None, None, "gx", "gy", "gz"),
            P("gx", None),
            P("gx", None),
            P("gx", None),
            P(),
            P(),
            P(),
            P("gx", "gy", "gz", None, None),
        ),
        out_specs=P(None, "gx", "gy", "gz"),
        check_vma=False,
    )
```

time: 130 us -> 34.7 us (0.27)
  starting transfers between devices: 42.3 us -> 0 us
  Pallas kernels: 0 us -> 31.5 us
  waiting for transfers between devices: 29.4 us -> 0 us
  blocking collectives: 23.5 us -> 0 us
  local copies, waits for them, and re-layouts: 18.1 us -> 1.36 us
  matrix products: 9.75 us -> 0 us
  other arithmetic: 5.91 us -> 1.63 us
    ppermute x24 -> x0, starting transfers between devices: 42.3 us -> none  [the longest x12 22.3 us: extended(): lax.ppermute(tail, axis, [(i, (i + 1) % count) for i in range(ends)])]
    pallas_call x0 -> x1, Pallas kernels: none -> 31.5 us  [local(): pl.pallas_call(functools.partial(kernel, sizes), out_shape=jax.ShapeDtype...]
    ppermute x24 -> x0, waiting for transfers between devices: 29.4 us -> none  [the longest x12 19 us: extended(): lax.ppermute(tail, axis, [(i, (i + 1) % count) for i in range(ends)])]
    all_gather x5 -> x0, blocking collectives: 23.5 us -> none  [the longest x4 18.4 us: interface_sum(): lax.all_gather(edge_values, 'gx', axis=0, tiled=True)]
    dot_general x24 -> x0, matrix products: 9.75 us -> none  [the longest x2 2.51 us: spread_back(): return jnp.einsum('sx,scyz->cxyz', select, expanded, precision=high)]
    slice x14 -> x0, local copies, waits for them, and re-layouts: 5.17 us -> none  [the longest x12 3.04 us: extended(): head = lax.slice_in_dim(cells, 0, width, axis=dim)]
    ppermute x4 -> x0, local copies, waits for them, and re-layouts: 4.81 us -> none  [the longest x2 3.3 us: extended(): lax.ppermute(head, axis, [((i + 1) % count, i) for i in range(ends)])]
    reshape x2 -> x0, local copies, waits for them, and re-layouts: 1.68 us -> none  [windows_of(): plane_rows.reshape(plane_rows.shape[0], 3, plane_rows.shape[2], plane_row...]
  transfers between devices with their start and end apart: 24 -> 0, of which waited for: 9 -> 0; matrix products, arithmetic and copies ran while one was open for 15% -> 0% of each run, Pallas kernels for 0% -> 0%
where the time goes in v1:
time: 34.7 us; the launch traced here: 34.5 us
  Pallas kernels  31.5 us (91%)
  other arithmetic  1.63 us (5%)
  local copies, waits for them, and re-layouts  1.36 us (4%)
    pallas_call x1, Pallas kernels, local(): pl.pallas_call(functools.partial(kernel, sizes), out_shape=jax.ShapeDtype...  31.5 us
    add x1, other arithmetic, local(): return pulled + direction  1.63 us
    unnamed x5, local copies, waits for them, and re-layouts  1.36 us

profile of v1, /device:TPU:0, one launch (start us, length us, event | category | flops | bytes accessed | tf_op | source)
XLA Modules:
  0.0 34.5 jit_solution(4419663155341594721)
XLA Ops:
  0.0 0.0 copy-start.1
  0.0 0.7 %copy-done.1 = f32[16,2]{0,1:T(2,128)S(1)} copy-done((f32[16,2]{0,1:T(2,128)S(1)}, f32[16,2]{0,1:T(2,128)}, u32[]{:S(2)}) %copy-start.1) | copy-done | bytes 152
  0.7 0.7 %copy.10.out_s = f32[16,2]{1,0:T(8,128)} copy(f32[16,2]{0,1:T(2,128)S(1)} %copy-done.1) | data formatting | bytes 256 | tf_op args[4]
  1.4 0.0 copy-start
  1.4 31.5 %shard_map.91 = f32[3,16,8,128]{3,2,1,0:T(8,128)} custom-call(f32[3,16,8,128]{3,2,1,0:T(8,128)} %dir_ref.1, bf16[2,3,16,8,128]{4,3,2,1,0:T(8,128)(2,1)} %base_ref.1, f32[4,16,16]{2,1,0:T(8,128)} %bitcast.1, f32[16,16]{1,0:T(8,128)} %local_s.1, f32[2,16]{1,0:T(2,128)} %in_s.1, f32[16,2]{1,0:T(8,128)} %copy.10.out_s, f32[4,4]{1,0:T(4,128)} %schur_s.1, ...), custom_call_target="tpu_custom_call" | custom-call | tf_op jit(solution)/shard_map/pallas_call | solution.py:401
  32.9 0.0 copy-done
  32.9 1.6 %add.3 = f32[3,16,8,128]{3,2,1,0:T(8,128)} add(f32[3,16,8,128]{3,2,1,0:T(8,128)} %shard_map.91, f32[3,16,8,128]{3,2,1,0:T(8,128)S(1)} %copy-done) | non-fusion elementwise | flops 49152 | bytes 589824 | tf_op jit(solution)/shard_map/add | solution.py:426
Async XLA Ops:
  0.0 0.7 %copy-start.1 = (f32[16,2]{0,1:T(2,128)S(1)}, f32[16,2]{0,1:T(2,128)}, u32[]{:S(2)}) copy-start(f32[16,2]{0,1:T(2,128)} %param.13) | copy-start | bytes 388
  1.4 31.5 %copy-start = (f32[3,16,8,128]{3,2,1,0:T(8,128)S(1)}, f32[3,16,8,128]{3,2,1,0:T(8,128)}, u32[]{:S(2)}) copy-start(f32[3,16,8,128]{3,2,1,0:T(8,128)} %dir_ref.1) | copy-start | bytes 589828

commit v2 on v1

--- a/solution.py
+++ b/solution.py
@@ -28,9 +28,10 @@
 
 def kernel(
     sizes,
-    dir_ref, base_ref, inv_ref,
-    local_s, in_s, out_s, schur_s, plane_s, slot_s,
+    dir_hbm, base_hbm, inv_hbm,
+    local_h, in_h, out_h, schur_h, plane_h, slot_h,
     res_ref,
+    dir_ref, base_ref, inv_ref, local_s, in_s, out_s, schur_s, plane_s, slot_s, load_sem,
     state_one, state_two, force, acc, rhs, obs, prod_y, prod_z, hbuf,
     yside, xrecv, ysend, yrecv, zsend, zrecv, edge, winrecv, lanes_inv, blocks,
     xs_sem, xr_sem, ys_sem, yr_sem, zs_sem, zr_sem, es_sem, er_sem, ws_sem, wr_sem,
@@ -38,7 +39,15 @@
     n_gx, n_gy, n_gz = sizes
     gx, gy, gz = lax.axis_index("gx"), lax.axis_index("gy"), lax.axis_index("gz")
     comps, cx, cy, cz = dir_ref.shape
-    half = ysend.shape[4]
+    wide = ysend.shape[2]
+    loads = [
+        pltpu.make_async_copy(src, dst, load_sem.at[n])
+        for n, (src, dst) in enumerate((
+            (dir_hbm, dir_ref), (in_h, in_s), (schur_h, schur_s), (local_h, local_s),
+            (out_h, out_s), (plane_h, plane_s), (slot_h, slot_s),
+            (base_hbm, base_ref), (inv_hbm, inv_ref),
+        ))
+    ]
     owned = inv_ref.shape[0]
     y_next, y_prev = lax.rem(gy + 1, n_gy), lax.rem(gy + n_gy - 1, n_gy)
     z_next, z_prev = lax.rem(gz + 1, n_gz), lax.rem(gz + n_gz - 1, n_gz)
@@ -59,6 +68,9 @@
     for q in (z_prev, z_next):
         pl.semaphore_signal(barrier, device_id={"gz": q}, device_id_type=MESH)
 
+    for copy in loads:
+        copy.start()
+
     def remote(src, dst, send, recv, where):
         return pltpu.make_async_remote_copy(
             src_ref=src, dst_ref=dst, send_sem=send, recv_sem=recv,
@@ -142,8 +154,11 @@
             copy.wait_recv()
 
     def pack_y(r, src):
-        ysend[r, 0] = src[:, :, 0:half, :]
-        ysend[r, 1] = src[:, :, cy - half : cy, :]
+        lines = src.reshape(comps * cx * cy, cz)
+        for c in range(comps):
+            for m in range(wide):
+                for side, row in ((0, m), (1, cy - wide + m)):
+                    ysend[r, side, m, c] = lines[pl.ds(c * cx * cy + row, cx, stride=cy), :]
 
     def pack_z(r, src):
         packed = None
@@ -177,8 +192,11 @@
         return jnp.where((lane < 3) | (lane >= cz - 3), turned, 0.0)
 
     def fill_sides(r):
-        yside[:, :, 0:half, :] = yrecv[r, 0]
-        yside[:, :, cy - half : cy, :] = yrecv[r, 1]
+        lines = yside.reshape(comps * cx * cy, cz)
+        for c in range(comps):
+            for m in range(wide):
+                for side, row in ((0, m), (1, cy - wide + m)):
+                    lines[pl.ds(c * cx * cy + row, cx, stride=cy), :] = yrecv[r, side, m, c]
 
     def along_y(block, side):
         def diff(k):
@@ -276,7 +294,9 @@
 
     def tangent(r, n, src, dst, first, shadow):
         xc, yc, zc, ec = x_copies(r, src), y_copies(r), z_copies(r), edge_copies(r)
-        if not first:
+        if first:
+            loads[0].wait()
+        else:
             x_start(xc)
         pack_z(r, src)
         if not first:
@@ -288,6 +308,9 @@
             start(zc)
         start(yc)
         sent.append((xc, yc + zc + ec))
+        if first:
+            for copy in loads[1:]:
+                copy.wait()
         for i in range(cx):
             block = src[:, i]
             acc[:, i] = block - time_step * (velocity(n, 2, i) * circular_z(block))
@@ -312,7 +335,7 @@
         arrived(ec)
         values = [interface(r, m, False) for m in range(2)]
         for i in range(cx):
-            pulled = out_s[i, 0] * values[0] + out_s[i, 1] * values[1]
+            pulled = out_s[0, i] * values[0] + out_s[1, i] * values[1]
             dst[:, i] = acc[:, i] - time_step * (
                 velocity(n, 0, i) * pulled + velocity(n, 2, i) * z_fix_of(fix, i)
             )
@@ -327,7 +350,7 @@
             prod_y[:, i] = velocity(n, 1, i) * block
             prod_z[:, i] = velocity(n, 2, i) * block
         for k in range(2):
-            edge[r, 0, k] = weighted([(out_s[i, k], rhs[:, i]) for i in range(cx)])
+            edge[r, 0, k] = weighted([(out_s[k, i], rhs[:, i]) for i in range(cx)])
         start(ec)
         pack_z(r, prod_z)
         start(zc)
@@ -389,7 +412,7 @@
         n_gx = sizes[0]
         comps, cx, cy, cz = direction.shape
         owned, count = window_inv.shape[0], window_inv.shape[3]
-        half = max(3, cy // 2)
+        wide = 3
         field = pltpu.VMEM(direction.shape, jnp.float32)
 
         def held(*shape):
@@ -397,18 +420,21 @@
 
         sems = pltpu.SemaphoreType.DMA
         vmem = pl.BlockSpec(memory_space=pltpu.VMEM)
-        smem = pl.BlockSpec(memory_space=pltpu.SMEM)
+        hbm = pl.BlockSpec(memory_space=pltpu.HBM)
+        tables = (local_inv, couple_in, couple_out.T, schur_inv, plane_x, slot_plane)
         pulled = pl.pallas_call(
             functools.partial(kernel, sizes),
             out_shape=jax.ShapeDtypeStruct(direction.shape, jnp.float32),
-            in_specs=[vmem] * 3 + [smem] * 6,
+            in_specs=[hbm] * 9,
             out_specs=vmem,
-            scratch_shapes=[field] * 8 + [
+            scratch_shapes=[
+                field, pltpu.VMEM(base_flow.shape, base_flow.dtype), held(owned, count, count),
+            ] + [pltpu.SMEM(t.shape, t.dtype) for t in tables] + [sems((9,))] + [field] * 8 + [
                 held(2, comps, cx, cy, cz),
                 field,
                 held(4, 2, comps, 2, cy, cz),
-                held(4, 2, comps, cx, half, cz),
-                held(4, 2, comps, cx, half, cz),
+                held(4, 2, wide, comps, cx, cz),
+                held(4, 2, wide, comps, cx, cz),
                 held(4, comps, cy, cz),
                 held(4, 2, comps, cy, cz),
                 held(4, n_gx, 2, comps, cy, cz),
@@ -421,7 +447,7 @@
             compiler_params=pltpu.CompilerParams(collective_id=0, has_side_effects=True),
         )(
             direction, base_flow, window_inv.reshape(owned, count, count),
-            local_inv, couple_in, couple_out, schur_inv, plane_x, slot_plane,
+            *tables,
         )
         return pulled + direction
 

time: 34.7 us -> 32.3 us (0.931)
  local copies, waits for them, and re-layouts: 1.36 us -> 0.01 us
  Pallas kernels: 31.5 us -> 30.5 us
    unnamed x5 -> x2, local copies, waits for them, and re-layouts: 1.36 us -> 0.01 us
    pallas_call x1, Pallas kernels: 31.5 us -> 30.5 us  [local(): pl.pallas_call(functools.partial(kernel, sizes), out_shape=jax.ShapeDtype...]
where the time goes in v2:
time: 32.3 us; the launch traced here: 32.1 us
  Pallas kernels  30.5 us (94%)
  other arithmetic  1.63 us (5%)
    pallas_call x1, Pallas kernels, local(): pl.pallas_call(functools.partial(kernel, sizes), out_shape=jax.ShapeDtype...  30.5 us
    add x1, other arithmetic, local(): return pulled + direction  1.63 us

profile of v2, /device:TPU:0, one launch (start us, length us, event | category | flops | bytes accessed | tf_op | source)
XLA Modules:
  0.0 32.1 jit_solution(12828806703054419961)
XLA Ops:
  0.0 0.0 copy-start
  0.0 30.5 %shard_map.91 = f32[3,16,8,128]{3,2,1,0:T(8,128)} custom-call(f32[3,16,8,128]{3,2,1,0:T(8,128)} %dir_hbm.1, bf16[2,3,16,8,128]{4,3,2,1,0:T(8,128)(2,1)} %base_hbm.1, f32[4,16,16]{2,1,0:T(8,128)} %bitcast.2, f32[16,16]{1,0:T(8,128)} %local_h.1, f32[2,16]{1,0:T(2,128)} %in_h.1, f32[2,16]{1,0:T(2,128)} %bitcast.3, f32[4,4]{1,0:T(4,128)} %schur_h.1, s32[8]{0:T(128)} %plane_h.1, ...), custom_call_target="tpu_custom_call" | custom-call | tf_op jit(solution)/shard_map/pallas_call | solution.py:425
  30.5 0.0 copy-done
  30.5 1.6 %add.3 = f32[3,16,8,128]{3,2,1,0:T(8,128)} add(f32[3,16,8,128]{3,2,1,0:T(8,128)} %shard_map.91, f32[3,16,8,128]{3,2,1,0:T(8,128)S(1)} %copy-done) | non-fusion elementwise | flops 49152 | bytes 589824 | tf_op jit(solution)/shard_map/add | solution.py:452
Async XLA Ops:
  0.0 30.5 %copy-start = (f32[3,16,8,128]{3,2,1,0:T(8,128)S(1)}, f32[3,16,8,128]{3,2,1,0:T(8,128)}, u32[]{:S(2)}) copy-start(f32[3,16,8,128]{3,2,1,0:T(8,128)} %dir_hbm.1) | copy-start | bytes 589828

commit v3 on v2

--- a/solution.py
+++ b/solution.py
@@ -31,7 +31,7 @@
     dir_hbm, base_hbm, inv_hbm,
     local_h, in_h, out_h, schur_h, plane_h, slot_h,
     res_ref,
-    dir_ref, base_ref, inv_ref, local_s, in_s, out_s, schur_s, plane_s, slot_s, load_sem,
+    dir_ref, base_ref, inv_ref, local_s, in_s, out_s, schur_s, plane_s, slot_s, in_v, near_v, near_s, esend, halo, load_sem, table_sem, ts_sem, tr_sem,
     state_one, state_two, force, acc, rhs, obs, prod_y, prod_z, hbuf,
     yside, xrecv, ysend, yrecv, zsend, zrecv, edge, winrecv, lanes_inv, blocks,
     xs_sem, xr_sem, ys_sem, yr_sem, zs_sem, zr_sem, es_sem, er_sem, ws_sem, wr_sem,
@@ -45,7 +45,7 @@
         for n, (src, dst) in enumerate((
             (dir_hbm, dir_ref), (in_h, in_s), (schur_h, schur_s), (local_h, local_s),
             (out_h, out_s), (plane_h, plane_s), (slot_h, slot_s),
-            (base_hbm, base_ref), (inv_hbm, inv_ref),
+            (base_hbm, base_ref), (inv_hbm, inv_ref), (in_h, in_v),
         ))
     ]
     owned = inv_ref.shape[0]
@@ -144,6 +144,14 @@
         remote(inv_ref, winrecv.at[d - 1], ws_sem.at[d], wr_sem.at[d], {"gx": lax.rem(gx + d, n_gx)})
         for d in range(1, n_gx)
     )
+
+    table_copies = (
+        remote(in_v, near_v.at[0], ts_sem.at[0], tr_sem.at[0], {"gx": lax.rem(gx + 1, n_gx)}),
+        remote(in_v, near_v.at[1], ts_sem.at[1], tr_sem.at[1], {"gx": lax.rem(gx + n_gx - 1, n_gx)}),
+    )
+    left_one = jnp.where(gx > 0, 1.0, 0.0)
+    right_one = jnp.where(gx < n_gx - 1, 1.0, 0.0)
+    left_id, right_id = lax.rem(gx + n_gx - 1, n_gx), lax.rem(gx + 1, n_gx)
 
     def start(copies):
         for copy in copies:
@@ -206,15 +214,23 @@
 
         return C1 * diff(1) + C2 * diff(2) + C3 * diff(3)
 
-    def stencil_x(src, r, i):
+    def stencil_x(src, sides, i):
         def row(n):
             if n < 0:
-                return xrecv[r, 0, :, n + 2]
+                return sides[0, :, n + 2]
             if n >= cx:
-                return xrecv[r, 1, :, n - cx]
+                return sides[1, :, n - cx]
             return src[:, n]
 
         return NEAR * (row(i + 1) - row(i - 1)) + FAR * (row(i + 2) - row(i - 2))
+
+    def stencil_inside(src, i):
+        total = None
+        for offset, coef in ((1, NEAR), (-1, -NEAR), (2, FAR), (-2, -FAR)):
+            if 0 <= i + offset < cx:
+                part = coef * src[:, i + offset]
+                total = part if total is None else total + part
+        return total
 
     def velocity(n, c, i):
         return base_ref[n, c, i].astype(jnp.float32)[None]
@@ -280,20 +296,49 @@
 
         lax.fori_loop(0, n_gx * owned, add_slot, 0)
 
-    def interface(r, m, transposed):
+    def interface(r, block, m, transposed):
         terms = []
         for d in range(n_gx):
             owner = lax.rem(gx + n_gx - d, n_gx)
             for k in range(2):
-                n, own = 2 * owner + k, 2 * gx + m
+                n, own = 2 * owner + k, 2 * block + m
                 coef = schur_s[n, own] if transposed else schur_s[own, n]
                 terms.append((coef, edge[r, d, k]))
         return weighted(terms)
 
+    def early_copies(r):
+        return tuple(
+            remote(esend.at[d], edge.at[r, d], es_sem.at[r, d], er_sem.at[r, d],
+                   {"gx": lax.rem(gx + d, n_gx)})
+            for d in range(1, n_gx)
+        )
+
+    def early_shares(r, src):
+        for i in range(cx):
+            rhs[:, i] = stencil_inside(src, i)
+        below = (NEAR * src[:, 0] + FAR * src[:, 1], FAR * src[:, 0])
+        above = (-(NEAR * src[:, cx - 1] + FAR * src[:, cx - 2]), -FAR * src[:, cx - 1])
+        parts = []
+        for k in range(2):
+            parts.append((2 * gx + k, weighted([(in_s[k, j], rhs[:, j]) for j in range(cx)])))
+            parts.append((2 * right_id + k, right_one * (
+                near_s[1, k, 0] * above[0] + near_s[1, k, 1] * above[1])))
+            parts.append((2 * left_id + k, left_one * (
+                near_s[0, k, cx - 1] * below[0] + near_s[0, k, cx - 2] * below[1])))
+        for d in tuple(range(1, n_gx)) + (0,):
+            owner = lax.rem(gx + d, n_gx)
+            for m in range(2):
+                share = weighted([(schur_s[2 * owner + m, n], part) for n, part in parts])
+                if d == 0:
+                    edge[r, 0, m] = share
+                else:
+                    esend[d, m] = share
+
     sent = []
 
     def tangent(r, n, src, dst, first, shadow):
-        xc, yc, zc, ec = x_copies(r, src), y_copies(r), z_copies(r), edge_copies(r)
+        xc, yc, zc = x_copies(r, src), y_copies(r), z_copies(r)
+        ec = edge_copies(r) if first else early_copies(r)
         if first:
             loads[0].wait()
         else:
@@ -307,24 +352,33 @@
             x_start(xc)
             start(zc)
         start(yc)
+        if not first:
+            early_shares(r, src)
+            start(ec)
         sent.append((xc, yc + zc + ec))
         if first:
             for copy in loads[1:]:
                 copy.wait()
+            start(table_copies)
         for i in range(cx):
             block = src[:, i]
             acc[:, i] = block - time_step * (velocity(n, 2, i) * circular_z(block))
         x_arrived(xc)
-        for i in range(cx):
-            rhs[:, i] = stencil_x(src, r, i)
-        for k in range(2):
-            edge[r, 0, k] = weighted([(in_s[k, j], rhs[:, j]) for j in range(cx)])
-        start(ec)
+        for i in range(cx) if first else (0, 1, cx - 2, cx - 1):
+            rhs[:, i] = stencil_x(src, xrecv.at[r], i)
         if first:
+            for k in range(2):
+                edge[r, 0, k] = weighted([(in_s[k, j], rhs[:, j]) for j in range(cx)])
+            start(ec)
             start(win_copies)
         for i in range(cx):
             solved = weighted([(local_s[i, j], rhs[:, j]) for j in range(cx)])
             acc[:, i] -= time_step * (velocity(n, 0, i) * solved)
+        if first:
+            arrived(table_copies)
+            table = pltpu.make_async_copy(near_v, near_s, table_sem.at[0])
+            table.start()
+            table.wait()
         shadow()
         arrived(yc)
         fill_sides(r)
@@ -333,7 +387,10 @@
         arrived(zc)
         fix = z_fix(r)
         arrived(ec)
-        values = [interface(r, m, False) for m in range(2)]
+        if first:
+            values = [interface(r, gx, m, False) for m in range(2)]
+        else:
+            values = [weighted([(1.0, edge[r, d, m]) for d in range(n_gx)]) for m in range(2)]
         for i in range(cx):
             pulled = out_s[0, i] * values[0] + out_s[1, i] * values[1]
             dst[:, i] = acc[:, i] - time_step * (
@@ -357,31 +414,37 @@
         pack_y(r, prod_y)
         start(yc)
         order = (0, 1, cx - 2, cx - 1) + tuple(range(2, cx - 2))
-        for i in order:
-            acc[:, i] = weighted([(local_s[j, i], rhs[:, j]) for j in range(cx)])
-        arrived(ec)
-        values = [interface(r, m, True) for m in range(2)]
         for place, i in enumerate(order):
-            held[:, i] = acc[:, i] + (in_s[0, i] * values[0] + in_s[1, i] * values[1])
+            held[:, i] = weighted([(local_s[j, i], rhs[:, j]) for j in range(cx)])
             if place == 3:
                 x_start(xc)
         for i in range(cx):
             total = src[:, i] + time_step * circular_z(prod_z[:, i])
             acc[:, i] = total if extra is None else total + extra[:, i]
+        arrived(ec)
+        values = [interface(r, gx, m, True) for m in range(2)]
+        lower = [left_one * interface(r, left_id, m, True) for m in range(2)]
+        upper = [right_one * interface(r, right_id, m, True) for m in range(2)]
+        for i in range(cx):
+            rhs[:, i] = held[:, i] + (in_s[0, i] * values[0] + in_s[1, i] * values[1])
         for i in range(2, cx - 2):
-            acc[:, i] += time_step * stencil_x(held, r, i)
+            acc[:, i] += time_step * stencil_x(rhs, halo, i)
+        x_arrived(xc)
+        for n in range(2):
+            halo[0, :, n] = xrecv[r, 0, :, n] + (
+                near_s[0, 0, cx - 2 + n] * lower[0] + near_s[0, 1, cx - 2 + n] * lower[1])
+            halo[1, :, n] = xrecv[r, 1, :, n] + (
+                near_s[1, 0, n] * upper[0] + near_s[1, 1, n] * upper[1])
+        for i in (0, 1, cx - 2, cx - 1):
+            acc[:, i] += time_step * stencil_x(rhs, halo, i)
         arrived(yc)
         fill_sides(r)
         for i in range(cx):
             acc[:, i] += time_step * along_y(prod_y[:, i], yside[:, i])
         arrived(zc)
         fix = z_fix(r)
-        x_arrived(xc)
-        for i in range(cx):
-            total = acc[:, i] + time_step * z_fix_of(fix, i)
-            if i < 2 or i >= cx - 2:
-                total = total + time_step * stencil_x(held, r, i)
-            dst[:, i] = total
+        for i in range(cx):
+            dst[:, i] = acc[:, i] + time_step * z_fix_of(fix, i)
 
     def nothing():
         pass
@@ -400,7 +463,7 @@
         x_sent(xc)
         for copy in rest:
             copy.wait_send()
-    for copy in win_copies:
+    for copy in win_copies + table_copies:
         copy.wait_send()
 
 
@@ -429,7 +492,11 @@
             out_specs=vmem,
             scratch_shapes=[
                 field, pltpu.VMEM(base_flow.shape, base_flow.dtype), held(owned, count, count),
-            ] + [pltpu.SMEM(t.shape, t.dtype) for t in tables] + [sems((9,))] + [field] * 8 + [
+            ] + [pltpu.SMEM(t.shape, t.dtype) for t in tables] + [
+                held(2, cx), held(2, 2, cx), pltpu.SMEM((2, 2, cx), jnp.float32),
+                held(n_gx, 2, comps, cy, cz), held(2, comps, 2, cy, cz),
+                sems((10,)), sems((1,)), sems((2,)), sems((2,)),
+            ] + [field] * 8 + [
                 held(2, comps, cx, cy, cz),
                 field,
                 held(4, 2, comps, 2, cy, cz),

time: 32.3 us -> 28.3 us (0.88)
  Pallas kernels: 30.5 us -> 26.5 us
    pallas_call x1, Pallas kernels: 30.5 us -> 26.5 us  [local(): pl.pallas_call(functools.partial(kernel, sizes), out_shape=jax.ShapeDtype...]
where the time goes in v3:
time: 28.3 us; the launch traced here: 28.2 us
  Pallas kernels  26.5 us (94%)
  other arithmetic  1.63 us (6%)
    pallas_call x1, Pallas kernels, local(): pl.pallas_call(functools.partial(kernel, sizes), out_shape=jax.ShapeDtype...  26.5 us
    add x1, other arithmetic, local(): return pulled + direction  1.63 us

profile of v3, /device:TPU:0, one launch (start us, length us, event | category | flops | bytes accessed | tf_op | source)
XLA Modules:
  0.0 28.2 jit_solution(14376582700634861390)
XLA Ops:
  0.0 0.0 copy-start
  0.0 26.5 %shard_map.91 = f32[3,16,8,128]{3,2,1,0:T(8,128)} custom-call(f32[3,16,8,128]{3,2,1,0:T(8,128)} %dir_hbm.1, bf16[2,3,16,8,128]{4,3,2,1,0:T(8,128)(2,1)} %base_hbm.1, f32[4,16,16]{2,1,0:T(8,128)} %bitcast.2, f32[16,16]{1,0:T(8,128)} %local_h.1, f32[2,16]{1,0:T(2,128)} %in_h.1, f32[2,16]{1,0:T(2,128)} %bitcast.3, f32[4,4]{1,0:T(4,128)} %schur_h.1, s32[8]{0:T(128)} %plane_h.1, ...), custom_call_target="tpu_custom_call" | custom-call | tf_op jit(solution)/shard_map/pallas_call | solution.py:488
  26.6 0.0 copy-done
  26.6 1.6 %add.3 = f32[3,16,8,128]{3,2,1,0:T(8,128)} add(f32[3,16,8,128]{3,2,1,0:T(8,128)} %shard_map.91, f32[3,16,8,128]{3,2,1,0:T(8,128)S(1)} %copy-done) | non-fusion elementwise | flops 49152 | bytes 589824 | tf_op jit(solution)/shard_map/add | solution.py:519
Async XLA Ops:
  0.0 26.6 %copy-start = (f32[3,16,8,128]{3,2,1,0:T(8,128)S(1)}, f32[3,16,8,128]{3,2,1,0:T(8,128)}, u32[]{:S(2)}) copy-start(f32[3,16,8,128]{3,2,1,0:T(8,128)} %dir_hbm.1) | copy-start | bytes 589828

commit v4 on v3

--- a/solution.py
+++ b/solution.py
@@ -402,17 +402,18 @@
         sent.append((xc, yc + zc + ec))
         held = hbuf.at[r - 2]
         for i in range(cx):
-            block = src[:, i]
-            rhs[:, i] = velocity(n, 0, i) * block
-            prod_y[:, i] = velocity(n, 1, i) * block
-            prod_z[:, i] = velocity(n, 2, i) * block
+            prod_z[:, i] = velocity(n, 2, i) * src[:, i]
+        pack_z(r, prod_z)
+        start(zc)
+        for i in range(cx):
+            prod_y[:, i] = velocity(n, 1, i) * src[:, i]
+        pack_y(r, prod_y)
+        start(yc)
+        for i in range(cx):
+            rhs[:, i] = velocity(n, 0, i) * src[:, i]
         for k in range(2):
             edge[r, 0, k] = weighted([(out_s[k, i], rhs[:, i]) for i in range(cx)])
         start(ec)
-        pack_z(r, prod_z)
-        start(zc)
-        pack_y(r, prod_y)
-        start(yc)
         order = (0, 1, cx - 2, cx - 1) + tuple(range(2, cx - 2))
         for place, i in enumerate(order):
             held[:, i] = weighted([(local_s[j, i], rhs[:, j]) for j in range(cx)])
@@ -483,6 +484,7 @@
 
         sems = pltpu.SemaphoreType.DMA
         vmem = pl.BlockSpec(memory_space=pltpu.VMEM)
+        kept = functools.partial(pltpu.with_memory_space_constraint, memory_space=pltpu.HBM)
         hbm = pl.BlockSpec(memory_space=pltpu.HBM)
         tables = (local_inv, couple_in, couple_out.T, schur_inv, plane_x, slot_plane)
         pulled = pl.pallas_call(
@@ -511,10 +513,9 @@
                 sems((4, 2)), sems((4, 2)), sems((4, 2)), sems((4, 2)), sems((4, 2)), sems((4, 2)),
                 sems((4, n_gx)), sems((4, n_gx)), sems((n_gx,)), sems((n_gx,)),
             ],
-            compiler_params=pltpu.CompilerParams(collective_id=0, has_side_effects=True),
+            compiler_params=pltpu.CompilerParams(collective_id=0, has_side_effects=True, vmem_limit_bytes=16 * 2**20),
         )(
-            direction, base_flow, window_inv.reshape(owned, count, count),
-            *tables,
+            *map(kept, (direction, base_flow, window_inv.reshape(owned, count, count)) + tables),
         )
         return pulled + direction
 

time: 28.3 us -> 26.6 us (0.940)
  other arithmetic: 1.63 us -> 0.7 us
  Pallas kernels: 26.5 us -> 25.7 us
    add x1, other arithmetic: 1.63 us -> 0.7 us  [local(): return pulled + direction]
    pallas_call x1, Pallas kernels: 26.5 us -> 25.7 us  [local(): pl.pallas_call(functools.partial(kernel, sizes), out_shape=jax.ShapeDtype...]
where the time goes in v4:
time: 26.6 us; the launch traced here: 26.4 us
  Pallas kernels  25.7 us (97%)
  other arithmetic  0.7 us (3%)
    pallas_call x1, Pallas kernels, local(): pl.pallas_call(functools.partial(kernel, sizes), out_shape=jax.ShapeDtype...  25.7 us
    add x1, other arithmetic, local(): return pulled + direction  0.7 us

profile of v4, /device:TPU:0, one launch (start us, length us, event | category | flops | bytes accessed | tf_op | source)
XLA Modules:
  0.0 26.4 jit_solution(11240678789099837477)
XLA Ops:
  0.0 0.0 copy-start
  0.0 25.7 %shard_map.91 = f32[3,16,8,128]{3,2,1,0:T(8,128)S(1)} custom-call(f32[3,16,8,128]{3,2,1,0:T(8,128)} %dir_hbm.1, bf16[2,3,16,8,128]{4,3,2,1,0:T(8,128)(2,1)} %base_hbm.1, f32[4,16,16]{2,1,0:T(8,128)} %bitcast.2, f32[16,16]{1,0:T(8,128)} %local_h.1, f32[2,16]{1,0:T(2,128)} %in_h.1, f32[2,16]{1,0:T(2,128)} %bitcast.3, f32[4,4]{1,0:T(4,128)} %schur_h.1, ...), custom_call_target="tpu_custom_call" | custom-call | tf_op jit(solution)/shard_map/pallas_call | solution.py:490
  25.7 0.0 copy-done
  25.7 0.7 %add.3 = f32[3,16,8,128]{3,2,1,0:T(8,128)} add(f32[3,16,8,128]{3,2,1,0:T(8,128)S(1)} %shard_map.91, f32[3,16,8,128]{3,2,1,0:T(8,128)S(1)} %copy-done) | non-fusion elementwise | flops 49152 | bytes 589824 | tf_op jit(solution)/shard_map/add | solution.py:520
Async XLA Ops:
  0.0 25.7 %copy-start = (f32[3,16,8,128]{3,2,1,0:T(8,128)S(1)}, f32[3,16,8,128]{3,2,1,0:T(8,128)}, u32[]{:S(2)}) copy-start(f32[3,16,8,128]{3,2,1,0:T(8,128)} %dir_hbm.1) | copy-start | bytes 589828
